TPU v7x, 32 devices: a whole 2x2x4 slice. The times are simulated.
32 devices in a mesh: rows: 4 (over y, x), mp: 8 (over z, core).
Axes of the slice: x: 2, y: 2, z: 4, core: 2. Of those that a mesh axis runs over, the one named last changes fastest.
Arguments:
- inputs: bfloat16 [8192, 2048], P(('rows', 'mp')), may hold values from -6 to 6
- cotangent: bfloat16 [8192, 2048], P(('rows', 'mp')), may hold values from -6 to 6
- corpus_ids: int32 [4], P('rows'), may hold values from 0 to 3
- corpus_weight: float32 [4], replicated, may hold values from 0.5 to 2
- attn_gain: bfloat16 [2048], P(('rows', 'mp')), may hold values from 0.099609375 to 1.8984375
- qkv_weight: bfloat16 [2048, 1920], P(('rows', 'mp')), may hold values from -0.125 to 0.125
- out_weight: bfloat16 [1280, 2048], P(('rows', 'mp')), may hold values from -2.5 to 2.5
- ffn_gain: bfloat16 [2048], P(('rows', 'mp')), may hold values from 0.099609375 to 1.8984375
- gate_weight: bfloat16 [2048, 6144], P(None, 'mp'), may hold values from -0.125 to 0.125
- up_weight: bfloat16 [2048, 6144], P(None, 'mp'), may hold values from -0.125 to 0.125
- down_weight: bfloat16 [6144, 2048], P('mp'), may hold values from -0.078125 to 0.078125
Outputs:
- outputs: bfloat16 [8192, 2048], P(('rows', 'mp'))
- input_grad: float32 [8192, 2048], P(('rows', 'mp'))
- qkv_grad: float32 [2048, 1920], P(('rows', 'mp'))
- proj_grad: float32 [1280, 2048], P(('rows', 'mp'))
- gate_grad: float32 [2048, 6144], P(None, 'mp')
- up_grad: float32 [2048, 6144], P(None, 'mp')
- down_grad: float32 [6144, 2048], P('mp')
- attn_gain_grad: float32 [2048], P(('rows', 'mp'))
- ffn_gain_grad: float32 [2048], P(('rows', 'mp'))
All inputs are finite; a program needn't handle non-finite values.
Results may differ from a plain program's by a relative error of at most 0.015.
Values may be sent and summed in bfloat16 or wider, within the bound.
A program may use at most 256 MiB of HBM per device.

v0:
```python
import jax
import jax.numpy as jnp
from jax import lax
from jax.sharding import PartitionSpec as P

HEADS = 20
KV_HEADS = 5
HEAD_DIM = 64
LEN = 2048
QBLOCK = 512
QBLOCKS = 4
EPS = 1e-05
THETA = 10000.0


def rotation(positions):
    half_dim = HEAD_DIM // 2
    freqs = jnp.exp(-jnp.log(THETA) * (2.0 * jnp.arange(half_dim, dtype=jnp.float32)) / HEAD_DIM)
    angles = positions.astype(jnp.float32)[:, None] * freqs[None, :]
    return (jnp.cos(angles), jnp.sin(angles))


def rotate(values_in, cosine, sine_part):
    half_dim = HEAD_DIM // 2
    first = values_in[..., :half_dim]
    second = values_in[..., half_dim:]
    return jnp.concatenate(
        [first * cosine - second * sine_part, second * cosine + first * sine_part], axis=-1
    )


def rotate_back(values_in, cosine, sine_part):
    half_dim = HEAD_DIM // 2
    first = values_in[..., :half_dim]
    second = values_in[..., half_dim:]
    return jnp.concatenate(
        [first * cosine + second * sine_part, second * cosine - first * sine_part], axis=-1
    )


def project_kv(normed, weight_kv, positions):
    row_count = normed.shape[0]
    kv_width = KV_HEADS * HEAD_DIM
    kv_raw = jnp.dot(normed, weight_kv, preferred_element_type=jnp.float32)
    cosine, sine_part = rotation(positions)
    keys_part = rotate(
        kv_raw[:, :kv_width].reshape(row_count, KV_HEADS, HEAD_DIM),
        cosine[:, None, :],
        sine_part[:, None, :],
    )
    return jnp.concatenate(
        [keys_part.reshape(row_count, kv_width), kv_raw[:, kv_width:]], axis=1
    ).astype(jnp.bfloat16)


def key_slices(kv_all, seq_start, kv_head, length):
    keys_part = lax.dynamic_slice(kv_all, (seq_start, kv_head * HEAD_DIM), (length, HEAD_DIM))
    values_part = lax.dynamic_slice(
        kv_all, (seq_start, (KV_HEADS + kv_head) * HEAD_DIM), (length, HEAD_DIM)
    )
    return (keys_part, values_part)


def masked_scores(queries, keys_part, block_index, length):
    scores = jnp.einsum(
        "qd,kd->qk", queries, keys_part, preferred_element_type=jnp.float32
    ) * HEAD_DIM ** (-0.5)
    allowed = jnp.arange(length)[None, :] <= block_index * QBLOCK + jnp.arange(QBLOCK)[:, None]
    return jnp.where(allowed, scores, -1e30)


def forward_branch(block_index):
    length = (block_index + 1) * QBLOCK

    def branch(queries, kv_all, seq_start, kv_head):
        keys_part, values_part = key_slices(kv_all, seq_start, kv_head, length)
        scores = masked_scores(queries, keys_part, block_index, length)
        row_max = jnp.max(scores, axis=1, keepdims=True)
        exponent = jnp.exp(scores - row_max)
        row_total = jnp.sum(exponent, axis=1, keepdims=True)
        probabilities = (exponent / row_total).astype(jnp.bfloat16)
        output = jnp.dot(probabilities, values_part, preferred_element_type=jnp.float32).astype(
            jnp.bfloat16
        )
        return (output, (row_max + jnp.log(row_total))[:, 0])

    return branch


def backward_branch(block_index):
    length = (block_index + 1) * QBLOCK

    def branch(queries, grad_output, log_total, kv_all, seq_start, kv_head):
        keys_part, values_part = key_slices(kv_all, seq_start, kv_head, length)
        scores = masked_scores(queries, keys_part, block_index, length)
        probabilities = jnp.exp(scores - log_total[:, None])
        grad_probs = jnp.einsum(
            "qd,kd->qk", grad_output, values_part, preferred_element_type=jnp.float32
        )
        row_delta = jnp.sum(probabilities * grad_probs, axis=1, keepdims=True)
        grad_scores = (probabilities * (grad_probs - row_delta)).astype(jnp.bfloat16)
        grad_queries = jnp.dot(
            grad_scores, keys_part, preferred_element_type=jnp.float32
        ) * HEAD_DIM ** (-0.5)
        grad_keys = jnp.einsum(
            "qk,qd->kd", grad_scores, queries, preferred_element_type=jnp.float32
        ) * HEAD_DIM ** (-0.5)
        grad_values = jnp.einsum(
            "qk,qd->kd",
            probabilities.astype(jnp.bfloat16),
            grad_output,
            preferred_element_type=jnp.float32,
        )
        padding = ((0, LEN - length), (0, 0))
        return (grad_queries, jnp.pad(grad_keys, padding), jnp.pad(grad_values, padding))

    return branch


def add_window(target, update, start_row, start_col):
    current = lax.dynamic_slice(target, (start_row, start_col), update.shape)
    return lax.dynamic_update_slice(target, current + update, (start_row, start_col))


def on_device(
    inputs,
    cotangent,
    corpus_ids,
    corpus_weight,
    attn_gain,
    qkv_weight,
    out_weight,
    ffn_gain,
    gate_weight,
    up_weight,
    down_weight,
):
    tok_dev = inputs.shape[0]
    group_rows = tok_dev * lax.axis_size("mp")
    offset = lax.axis_index("mp") * tok_dev
    seq_group = corpus_ids.shape[0]
    corpora_count = corpus_weight.shape[0]
    sequences_all = seq_group * lax.axis_size("rows")
    q_width = HEADS * HEAD_DIM
    kv_width = KV_HEADS * HEAD_DIM
    group_size = HEADS // KV_HEADS
    model_width = inputs.shape[1]
    tiles_dev = HEADS * QBLOCKS // lax.axis_size("mp")
    first_tile = lax.axis_index("mp") * tiles_dev
    chosen = (corpus_ids[:, None] == jnp.arange(corpora_count)[None, :]).astype(jnp.float32)
    counts = lax.psum(jnp.sum(chosen, axis=0), "rows")
    count_seq = jnp.sum(chosen * counts[None, :], axis=1)
    weight_seq = jnp.sum(chosen * corpus_weight[None, :], axis=1)
    seq_scale = weight_seq * sequences_all / (corpora_count * count_seq)
    qkv_full, out_full, gain_one, gain_two = (
        lax.all_gather(qkv_weight, ("rows", "mp"), axis=0, tiled=True),
        lax.all_gather(out_weight, ("rows", "mp"), axis=0, tiled=True),
        lax.all_gather(attn_gain, ("rows", "mp"), axis=0, tiled=True),
        lax.all_gather(ffn_gain, ("rows", "mp"), axis=0, tiled=True),
    )
    gain_one = gain_one.astype(jnp.float32)
    gain_two = gain_two.astype(jnp.float32)
    weight_kv = qkv_full[:, q_width:]
    residual = inputs.astype(jnp.float32)
    inverse_one = lax.rsqrt(jnp.mean(residual * residual, axis=-1, keepdims=True) + EPS)
    normed_one = (residual * inverse_one * gain_one).astype(jnp.bfloat16)
    local_pos = (offset + jnp.arange(tok_dev)) % LEN
    normed_all, kv_all = (
        lax.all_gather(normed_one, "mp", axis=0, tiled=True),
        lax.all_gather(project_kv(normed_one, weight_kv, local_pos), "mp", axis=0, tiled=True),
    )
    count_items = tiles_dev * seq_group
    forward_list = [forward_branch(b) for b in range(QBLOCKS)]
    backward_list = [backward_branch(b) for b in range(QBLOCKS)]

    def item_info(item_index):
        tile_index = first_tile + item_index // seq_group
        seq_start = item_index % seq_group * LEN
        head_index = tile_index // QBLOCKS
        block_index = tile_index % QBLOCKS
        return (head_index, block_index, seq_start, seq_start + block_index * QBLOCK)

    def forward_item(partial_value, item_index):
        head_index, block_index, seq_start, row_start = item_info(item_index)
        rows_in = lax.dynamic_slice(normed_all, (row_start, 0), (QBLOCK, model_width))
        weight_q = lax.dynamic_slice(qkv_full, (0, head_index * HEAD_DIM), (model_width, HEAD_DIM))
        raw_queries = jnp.dot(rows_in, weight_q, preferred_element_type=jnp.float32)
        cosine, sine_part = rotation(block_index * QBLOCK + jnp.arange(QBLOCK))
        queries = rotate(raw_queries, cosine, sine_part).astype(jnp.bfloat16)
        output, log_total = lax.switch(
            block_index, forward_list, queries, kv_all, seq_start, head_index // group_size
        )
        weight_o = lax.dynamic_slice(out_full, (head_index * HEAD_DIM, 0), (HEAD_DIM, model_width))
        partial_value = add_window(
            partial_value,
            jnp.dot(output, weight_o, preferred_element_type=jnp.float32),
            row_start,
            0,
        )
        return (partial_value, (queries, output, log_total))

    attn_partial, (kept_queries, kept_outputs, kept_totals) = lax.scan(
        forward_item, jnp.zeros((group_rows, model_width), jnp.float32), jnp.arange(count_items)
    )
    attn_sum = lax.psum_scatter(attn_partial, "mp", scatter_dimension=0, tiled=True)
    middle = residual + attn_sum
    inverse_two = lax.rsqrt(jnp.mean(middle * middle, axis=-1, keepdims=True) + EPS)
    normed_two = (middle * inverse_two * gain_two).astype(jnp.bfloat16)
    normed_mid = lax.all_gather(normed_two, "mp", axis=0, tiled=True)
    gate_val = jnp.dot(normed_mid, gate_weight, preferred_element_type=jnp.float32)
    up_val = jnp.dot(normed_mid, up_weight, preferred_element_type=jnp.float32)
    hidden = (jax.nn.silu(gate_val) * up_val).astype(jnp.bfloat16)
    ffn_part = jnp.dot(hidden, down_weight, preferred_element_type=jnp.float32)
    ffn_sum = lax.psum_scatter(
        ffn_part.astype(jnp.bfloat16), "mp", scatter_dimension=0, tiled=True
    ).astype(jnp.float32)
    outputs = (middle + ffn_sum).astype(jnp.bfloat16)
    seq_local = (offset + jnp.arange(tok_dev)) // LEN
    token_scale = jnp.sum(
        (seq_local[:, None] == jnp.arange(seq_group)[None, :]).astype(jnp.float32)
        * seq_scale[None, :],
        axis=1,
    )
    grad_out = cotangent.astype(jnp.float32) * token_scale[:, None]
    grad_all = lax.all_gather(grad_out.astype(jnp.bfloat16), "mp", axis=0, tiled=True)
    grad_hidden = jnp.einsum("td,fd->tf", grad_all, down_weight, preferred_element_type=jnp.float32)
    down_grad = jnp.einsum("tf,td->fd", hidden, grad_all, preferred_element_type=jnp.float32)
    sigmoid_val = jax.nn.sigmoid(gate_val)
    grad_gate = (
        grad_hidden * up_val * (sigmoid_val * (1.0 + gate_val * (1.0 - sigmoid_val)))
    ).astype(jnp.bfloat16)
    grad_up = (grad_hidden * (gate_val * sigmoid_val)).astype(jnp.bfloat16)
    gate_grad = jnp.einsum("td,tf->df", normed_mid, grad_gate, preferred_element_type=jnp.float32)
    up_grad = jnp.einsum("td,tf->df", normed_mid, grad_up, preferred_element_type=jnp.float32)
    mid_partial = jnp.einsum(
        "tf,df->td", grad_gate, gate_weight, preferred_element_type=jnp.float32
    )
    mid_partial = mid_partial + jnp.einsum(
        "tf,df->td", grad_up, up_weight, preferred_element_type=jnp.float32
    )
    grad_normed_two = lax.psum_scatter(mid_partial, "mp", scatter_dimension=0, tiled=True)
    scaled_two = grad_normed_two * gain_two
    ffn_gain_part = jnp.sum(grad_normed_two * middle * inverse_two, axis=0)
    grad_middle = (
        grad_out
        + inverse_two * scaled_two
        - middle * inverse_two**3 * jnp.mean(scaled_two * middle, axis=-1, keepdims=True)
    )
    grad_attn_all = lax.all_gather(grad_middle.astype(jnp.bfloat16), "mp", axis=0, tiled=True)

    def backward_item(carried, item_index):
        input_partial, kv_partial, q_grad_w, o_grad_w = carried
        head_index, block_index, seq_start, row_start = item_info(item_index)
        queries = kept_queries[item_index]
        output = kept_outputs[item_index]
        log_total = kept_totals[item_index]
        grad_rows = lax.dynamic_slice(grad_attn_all, (row_start, 0), (QBLOCK, model_width))
        weight_o = lax.dynamic_slice(out_full, (head_index * HEAD_DIM, 0), (HEAD_DIM, model_width))
        grad_output = jnp.einsum(
            "td,hd->th", grad_rows, weight_o, preferred_element_type=jnp.float32
        ).astype(jnp.bfloat16)
        o_grad_w = add_window(
            o_grad_w,
            jnp.einsum("th,td->hd", output, grad_rows, preferred_element_type=jnp.float32),
            head_index * HEAD_DIM,
            0,
        )
        kv_head = head_index // group_size
        grad_queries, grad_keys, grad_values = lax.switch(
            block_index, backward_list, queries, grad_output, log_total, kv_all, seq_start, kv_head
        )
        cosine, sine_part = rotation(block_index * QBLOCK + jnp.arange(QBLOCK))
        grad_raw = rotate_back(grad_queries, cosine, sine_part).astype(jnp.bfloat16)
        rows_in = lax.dynamic_slice(normed_all, (row_start, 0), (QBLOCK, model_width))
        weight_q = lax.dynamic_slice(qkv_full, (0, head_index * HEAD_DIM), (model_width, HEAD_DIM))
        input_partial = add_window(
            input_partial,
            jnp.einsum("th,dh->td", grad_raw, weight_q, preferred_element_type=jnp.float32),
            row_start,
            0,
        )
        q_grad_w = add_window(
            q_grad_w,
            jnp.einsum("td,th->dh", rows_in, grad_raw, preferred_element_type=jnp.float32),
            0,
            head_index * HEAD_DIM,
        )
        kv_partial = add_window(kv_partial, grad_keys, seq_start, kv_head * HEAD_DIM)
        kv_partial = add_window(kv_partial, grad_values, seq_start, (KV_HEADS + kv_head) * HEAD_DIM)
        return ((input_partial, kv_partial, q_grad_w, o_grad_w), None)

    start_state = (
        jnp.zeros((group_rows, model_width), jnp.float32),
        jnp.zeros((group_rows, 2 * kv_width), jnp.float32),
        jnp.zeros((model_width, q_width), jnp.float32),
        jnp.zeros((q_width, model_width), jnp.float32),
    )
    (input_partial, kv_partial, q_grad_w, o_grad_w), unused = lax.scan(
        backward_item, start_state, jnp.arange(count_items)
    )
    input_sum, kv_sum = (
        lax.psum_scatter(input_partial, "mp", scatter_dimension=0, tiled=True),
        lax.psum_scatter(kv_partial, "mp", scatter_dimension=0, tiled=True),
    )
    cos_local, sin_local = rotation(local_pos)
    grad_keys_local = rotate_back(
        kv_sum[:, :kv_width].reshape(tok_dev, KV_HEADS, HEAD_DIM),
        cos_local[:, None, :],
        sin_local[:, None, :],
    )
    grad_kv = jnp.concatenate(
        [grad_keys_local.reshape(tok_dev, kv_width), kv_sum[:, kv_width:]], axis=1
    ).astype(jnp.bfloat16)
    grad_normed_one = input_sum + jnp.einsum(
        "tk,dk->td", grad_kv, weight_kv, preferred_element_type=jnp.float32
    )
    kv_grad_w = jnp.einsum("td,tk->dk", normed_one, grad_kv, preferred_element_type=jnp.float32)
    qkv_grad_full = jnp.concatenate([q_grad_w, kv_grad_w], axis=1)
    scaled_one = grad_normed_one * gain_one
    attn_gain_part = jnp.sum(grad_normed_one * residual * inverse_one, axis=0)
    input_grad = (
        grad_middle
        + inverse_one * scaled_one
        - residual * inverse_one**3 * jnp.mean(scaled_one * residual, axis=-1, keepdims=True)
    )
    qkv_grad, proj_grad, attn_gain_grad, ffn_gain_grad = (
        lax.psum_scatter(qkv_grad_full, ("rows", "mp"), scatter_dimension=0, tiled=True),
        lax.psum_scatter(o_grad_w, ("rows", "mp"), scatter_dimension=0, tiled=True),
        lax.psum_scatter(attn_gain_part, ("rows", "mp"), scatter_dimension=0, tiled=True),
        lax.psum_scatter(ffn_gain_part, ("rows", "mp"), scatter_dimension=0, tiled=True),
    )
    gate_grad, up_grad, down_grad = (
        lax.psum(gate_grad.astype(jnp.bfloat16), "rows").astype(jnp.float32),
        lax.psum(up_grad.astype(jnp.bfloat16), "rows").astype(jnp.float32),
        lax.psum(down_grad.astype(jnp.bfloat16), "rows").astype(jnp.float32),
    )
    return (
        outputs,
        input_grad,
        qkv_grad,
        proj_grad,
        gate_grad,
        up_grad,
        down_grad,
        attn_gain_grad,
        ffn_gain_grad,
    )


def solution(mesh):
    in_specs = (
        P(("rows", "mp"), None),
        P(("rows", "mp"), None),
        P("rows"),
        P(),
        P(("rows", "mp")),
        P(("rows", "mp"), None),
        P(("rows", "mp"), None),
        P(("rows", "mp")),
        P(None, "mp"),
        P(None, "mp"),
        P("mp", None),
    )
    out_specs = (
        P(("rows", "mp"), None),
        P(("rows", "mp"), None),
        P(("rows", "mp"), None),
        P(("rows", "mp"), None),
        P(None, "mp"),
        P(None, "mp"),
        P("mp", None),
        P(("rows", "mp")),
        P(("rows", "mp")),
    )
    return jax.shard_map(
        on_device, mesh=mesh, in_specs=in_specs, out_specs=out_specs, check_vma=False
    )
```

profile of v0, /device:TPU:0, one launch (start us, length us, event | category | flops | bytes accessed | tf_op | source)
XLA Modules:
  0.0 2238.0 jit_solution(10643275704402246868)
XLA Ops:
  10.4 43.2 %all-reduce.11 = (bf16[2048]{0:T(1024)(128)(2,1)S(1)}, bf16[2048]{0:T(1024)(128)(2,1)S(1)}) all-reduce(bf16[2048]{0:T(1024)(128)(2,1)S(1)} %dynamic-update-slice, bf16[2048]{0:T(1024)(128)(2,1)S(1)} %dynamic-update-slice.1), channel_id=1, replica_groups=mesh['rows'=4,'mp'=8] {'rows','mp'}, use_global_device_ids=true, to_apply=%add.6 | all-reduce | flops 4096 | bytes 16384
  59.7 29.9 %all-gather.10.cloned.1.call-done = bf16[2048,1920]{1,0:T(8,128)(2,1)} async-done(((bf16[64,1920]{1,0:T(8,128)(2,1)}), bf16[2048,1920]{1,0:T(8,128)(2,1)}) %all-gather.10.cloned.1.call-update) | async-done | bytes 7864336 | tf_op jit(solution)/shard_map/all_gather | solution.py:156
  97.7 58.8 %all-gather.14.cloned.1.call-done = bf16[1280,2048]{1,0:T(8,128)(2,1)} async-done(((bf16[40,2048]{1,0:T(8,128)(2,1)}), bf16[1280,2048]{1,0:T(8,128)(2,1)}) %all-gather.14.cloned.1.call-update) | async-done | bytes 5242896 | tf_op jit(solution)/shard_map/all_gather | solution.py:157
  156.5 82.6 %all-gather.8.cloned.1.call-done = bf16[2048,2048]{1,0:T(8,128)(2,1)} async-done(((bf16[256,2048]{1,0:T(8,128)(2,1)}), bf16[2048,2048]{1,0:T(8,128)(2,1)}) %all-gather.8.cloned.1.call-update) | async-done | bytes 8388624 | tf_op jit(solution)/shard_map/all_gather | solution.py:169
  239.1 34.5 %all-gather.12.cloned.1.call-done = bf16[2048,640]{1,0:T(8,128)(2,1)} async-done(((bf16[256,640]{1,0:T(8,128)(2,1)}), bf16[2048,640]{1,0:T(8,128)(2,1)}) %all-gather.12.cloned.1.call-update) | async-done | bytes 2621456 | tf_op jit(solution)/shard_map/all_gather | solution.py:170
  273.6 7.9 broadcast.482.clone
  281.5 150.9 %while.42 = (s32[]{:T(128)}, f32[2048,2048]{1,0:T(8,128)}, bf16[10,512,64]{1,2,0:T(8,128)(2,1)}, bf16[10,512,64]{1,2,0:T(8,128)(2,1)}, f32[10,512]{1,0:T(8,128)S...) while((s32[]{:T(128)}, f32[2048,2048]{1,0:T(8,128)}, ...), condition=%wide.region_14.15_spmd, body=%wide.region_1.14_spmd.sunk | while | flops 547767360 | bytes 25982072 | solution.py:202
  314.9 5.5 conditional.17
  330.5 6.2 conditional.17
  375.8 5.5 conditional.17
  391.4 6.2 conditional.17
  432.5 169.8 %reduce-scatter.8.cloned.1.call-done = f32[256,2048]{1,0:T(8,128)} async-done(((f32[2048,2048]{1,0:T(8,128)}), f32[256,2048]{1,0:T(8,128)}) %reduce-scatter.8.cloned.1.call-update) | async-done | bytes 2097168 | tf_op jit(solution)/shard_map/reduce_scatter | solution.py:205
  607.7 9.9 psum.28
  622.9 64.7 %all-gather.16.cloned.1.call-done = bf16[2048,2048]{1,0:T(8,128)(2,1)} async-done(((bf16[256,2048]{1,0:T(8,128)(2,1)}), bf16[2048,2048]{1,0:T(8,128)(2,1)}) %all-gather.16.cloned.1.call-update) | async-done | bytes 8388624 | tf_op jit(solution)/shard_map/all_gather | solution.py:209
  687.6 11.8 fusion.167
  699.4 8.5 fusion.166
  707.9 62.5 %all-gather.18.cloned.1.call-done = bf16[2048,2048]{1,0:T(8,128)(2,1)} async-done(((bf16[256,2048]{1,0:T(8,128)(2,1)}), bf16[2048,2048]{1,0:T(8,128)(2,1)}) %all-gather.18.cloned.1.call-update) | async-done | bytes 8388624 | tf_op jit(solution)/shard_map/all_gather | solution.py:225
  770.4 15.7 multiply_convert_fusion.2
  786.1 13.3 fusion.168
  799.4 14.1 convolution_add_fusion.2
  813.6 10.8 convolution_convert_fusion
  824.5 156.0 %reduce-scatter.12.cloned.1.call-done = f32[256,2048]{1,0:T(8,128)} async-done(((f32[2048,2048]{1,0:T(8,128)}), f32[256,2048]{1,0:T(8,128)}) %reduce-scatter.12.cloned.1.call-update) | async-done | bytes 2097168 | tf_op jit(solution)/shard_map/reduce_scatter | solution.py:241
  983.3 87.6 %reduce-scatter.10.cloned.1.call-done = bf16[256,2048]{1,0:T(8,128)(2,1)} async-done(((bf16[2048,2048]{1,0:T(8,128)(2,1)}), bf16[256,2048]{1,0:T(8,128)(2,1)}) %reduce-scatter.10.cloned.1.call-update) | async-done | bytes 1048592 | tf_op jit(solution)/shard_map/reduce_scatter | solution.py:214
  1077.9 78.2 %all-gather.20.cloned.1.call-done = bf16[2048,2048]{1,0:T(8,128)(2,1)} async-done(((bf16[256,2048]{1,0:T(8,128)(2,1)}), bf16[2048,2048]{1,0:T(8,128)(2,1)}) %all-gather.20.cloned.1.call-update) | async-done | bytes 8388624 | tf_op jit(solution)/shard_map/all_gather | solution.py:249
  1164.3 5.3 broadcast_in_dim.138
  1169.6 7.9 broadcast.482
  1177.5 293.2 %while.43 = (s32[]{:T(128)}, f32[2048,2048]{1,0:T(8,128)}, f32[2048,640]{0,1:T(8,128)}, f32[2048,1280]{0,1:T(8,128)}, f32[1280,2048]{1,0:T(8,128)}, /*index=5*/s...) while((s32[]{:T(128)}, f32[2048,2048]{1,0:T(8,128)}, ...), condition=%wide.region_32.33_spmd, body=%wide.region_23.32_spmd.sunk | while | flops 1220625536 | bytes 55792484 | solution.py:298
  1183.3 6.6 conditional.18
  1210.8 7.9 conditional.18
  1239.8 9.2 conditional.18
  1270.0 10.5 conditional.18
  1301.4 6.6 conditional.18
  1329.0 7.9 conditional.18
  1357.9 9.2 conditional.18
  1388.1 10.5 conditional.18
  1419.5 6.6 conditional.18
  1447.1 7.9 conditional.18
  1470.7 12.2 convolution_convert_fusion.1
  1482.9 8.5 convolution_convert_fusion.2
  1491.4 8.5 convolution_convert_fusion.3
  1501.3 11.6 copy.61
  1512.9 21.2 reduce-scatter.16.cloned.1.call-done
  1540.1 6.3 pad_maximum_fusion.4
  1546.4 180.2 %all-reduce.15.cloned.1.call-done = (bf16[2048,768]{1,0:T(8,128)(2,1)}, bf16[2048,768]{1,0:T(8,128)(2,1)}, bf16[768,2048]{1,0:T(8,128)(2,1)}) async-done(((bf16[2048,768]{1,0:T(8,128)(2,1)}, bf16[2048,768]{1,0:T(8,128)(2,1)}, bf16[768,2048]{1,0:T(8,128)(2,1)}), (bf16[2048,768]{1,0:T(8,128)(2,1)}, bf16[2048,768]{1,0:T(8,128)(2,1)}, bf16[768,2048]{1,0:T(8,128)(2,1)})) %all-reduce.15.cloned.1.call-update) | async-done | bytes 9437200 | tf_op jit(solution)/shard_map/psum | solution.py:333
  1739.3 158.0 %reduce-scatter.14.cloned.1.call-done = f32[256,2048]{1,0:T(8,128)} async-done(((f32[2048,2048]{1,0:T(8,128)}), f32[256,2048]{1,0:T(8,128)}) %reduce-scatter.14.cloned.1.call-update) | async-done | bytes 2097168 | tf_op jit(solution)/shard_map/reduce_scatter | solution.py:302
  1902.3 38.8 %all-reduce.10 = (f32[2048]{0:T(1024)S(1)}, f32[2048]{0:T(1024)S(1)}) all-reduce(f32[2048]{0:T(1024)S(1)} %get-tuple-element.1396, f32[2048]{0:T(1024)S(1)} %copy-done.14), channel_id=9, replica_groups=mesh['rows'=4,'mp'=8] {'rows','mp'}, use_global_device_ids=true, to_apply=%region_42.43.clone | all-reduce | flops 4096 | bytes 32768
  1947.0 109.4 %reduce-scatter.20.cloned.1.call-done = f32[40,2048]{1,0:T(8,128)} async-done(((f32[1280,2048]{1,0:T(8,128)}), f32[40,2048]{1,0:T(8,128)}) %reduce-scatter.20.cloned.1.call-update) | async-done | bytes 327696 | tf_op jit(solution)/shard_map/reduce_scatter | solution.py:328
  2056.3 174.8 %reduce-scatter.18.cloned.1.call-done = f32[64,1920]{1,0:T(8,128)} async-done(((f32[2048,1920]{1,0:T(8,128)}), f32[64,1920]{1,0:T(8,128)}) %reduce-scatter.18.cloned.1.call-update) | async-done | bytes 491536 | tf_op jit(solution)/shard_map/reduce_scatter | solution.py:327
  (482 shorter events, 510.6 us)
Async XLA Ops:
  7.2 763.2 %copy-start = (bf16[768,2048]{1,0:T(8,128)(2,1)S(1)}, bf16[768,2048]{1,0:T(8,128)(2,1)}, u32[]{:S(2)}) copy-start(bf16[768,2048]{1,0:T(8,128)(2,1)} %param.33) | copy-start | bytes 9437188
  7.2 82.5 %all-gather.10.cloned.1.call-start = ((), (), s32[]{:S(2)}) async-start(), calls=%async_computation.8 | async-start | bytes 8110080 | tf_op jit(solution)/shard_map/all_gather | solution.py:156
  7.9 148.6 %all-gather.14.cloned.1.call-start = ((), (), s32[]{:S(2)}) async-start(), calls=%async_computation.10 | async-start | bytes 5406720 | tf_op jit(solution)/shard_map/all_gather | solution.py:157
  8.7 230.4 %all-gather.8.cloned.1.call-start = ((), (), s32[]{:S(2)}) async-start(), calls=%async_computation.7 | async-start | bytes 9437184 | tf_op jit(solution)/shard_map/all_gather | solution.py:169
  53.6 2.1 copy-start.12
  55.7 0.5 copy-start.15
  58.8 214.7 %all-gather.12.cloned.1.call-start = ((), (), s32[]{:S(2)}) async-start(), calls=%async_computation.9 | async-start | bytes 2949120 | tf_op jit(solution)/shard_map/all_gather | solution.py:170
  97.4 504.8 %reduce-scatter.8.cloned.1.call-start = ((), (), s32[]{:S(2)}) async-start(), calls=%async_computation.11 | async-start | bytes 18874368 | tf_op jit(solution)/shard_map/reduce_scatter | solution.py:205
  432.4 255.2 %all-gather.16.cloned.1.call-start = ((), (), s32[]{:S(2)}) async-start(), calls=%async_computation.12 | async-start | bytes 9437184 | tf_op jit(solution)/shard_map/all_gather | solution.py:209
  604.5 1.3 copy-start.3
  604.5 13.1 copy-start.23
  607.0 163.4 %all-gather.18.cloned.1.call-start = ((), (), s32[]{:S(2)}) async-start(), calls=%async_computation.14 | async-start | bytes 9437184 | tf_op jit(solution)/shard_map/all_gather | solution.py:225
  622.7 357.9 %reduce-scatter.12.cloned.1.call-start = ((), (), s32[]{:S(2)}) async-start(), calls=%async_computation.15 | async-start | bytes 18874368 | tf_op jit(solution)/shard_map/reduce_scatter | solution.py:241
  687.6 11.8 copy-start.18
  687.6 11.8 copy-start.20
  770.4 15.7 copy-start.21
  786.1 13.3 copy-start.24
  786.1 13.3 copy-start.22
  813.6 257.2 %reduce-scatter.10.cloned.1.call-start = ((), (), s32[]{:S(2)}) async-start(), calls=%async_computation.13 | async-start | bytes 9437184 | tf_op jit(solution)/shard_map/reduce_scatter | solution.py:214
  824.4 156.1 %copy-start.4 = (f32[256,2048]{1,0:T(8,128)S(1)}, f32[256,2048]{1,0:T(8,128)}, u32[]{:S(2)}) copy-start(f32[256,2048]{1,0:T(8,128)} %copy-done.3) | copy-start | bytes 6291460
  824.5 246.3 %copy-start.7 = (bf16[256,2048]{1,0:T(8,128)(2,1)S(1)}, bf16[256,2048]{1,0:T(8,128)(2,1)}, u32[]{:S(2)}) copy-start(bf16[256,2048]{1,0:T(8,128)(2,1)} %param.24) | copy-start | bytes 3145732
  824.5 331.6 %all-gather.20.cloned.1.call-start = ((), (), s32[]{:S(2)}) async-start(), calls=%async_computation.16 | async-start | bytes 9437184 | tf_op jit(solution)/shard_map/all_gather | solution.py:249
  1075.5 458.6 %reduce-scatter.16.cloned.1.call-start = ((), (), s32[]{:S(2)}) async-start(), calls=%async_computation.18 | async-start | bytes 5898240 | tf_op jit(solution)/shard_map/reduce_scatter | solution.py:303
  1470.7 12.2 copy-start.25
  1470.7 255.9 %all-reduce.15.cloned.1.call-start = ((), (), s32[]{:S(2)}) async-start(), calls=%async_computation.21 | async-start | bytes 18874368 | tf_op jit(solution)/shard_map/psum | solution.py:333
  1470.7 12.2 copy-start.19
  1482.9 8.5 copy-start.26
  1499.9 397.3 %reduce-scatter.14.cloned.1.call-start = ((), (), s32[]{:S(2)}) async-start(), calls=%async_computation.17 | async-start | bytes 18874368 | tf_op jit(solution)/shard_map/reduce_scatter | solution.py:302
  1500.7 555.7 %reduce-scatter.20.cloned.1.call-start = ((), (), s32[]{:S(2)}) async-start(), calls=%async_computation.20 | async-start | bytes 10813440 | tf_op jit(solution)/shard_map/reduce_scatter | solution.py:328
  1501.2 729.9 %reduce-scatter.18.cloned.1.call-start = ((), (), s32[]{:S(2)}) async-start(), calls=%async_computation.19 | async-start | bytes 16220160 | tf_op jit(solution)/shard_map/reduce_scatter | solution.py:327
  1501.3 34.8 %copy-start.10 = (f32[256,32]{0,1:T(8,128)S(1)}, f32[256,32]{0,1:T(8,128)}, u32[]{:S(2)}) copy-start(f32[256,32]{0,1:T(8,128)} %get-tuple-element.1491) | copy-start | bytes 98308
  1501.3 34.8 %copy-start.11 = (f32[256,32]{0,1:T(8,128)S(1)}, f32[256,32]{0,1:T(8,128)}, u32[]{:S(2)}) copy-start(f32[256,32]{0,1:T(8,128)} %get-tuple-element.1492) | copy-start | bytes 98308
  1501.3 34.9 %copy-start.6 = (bf16[256,2048]{1,0:T(8,128)(2,1)S(1)}, bf16[256,2048]{1,0:T(8,128)(2,1)}, u32[]{:S(2)}) copy-start(bf16[256,2048]{1,0:T(8,128)(2,1)} %fusion.148) | copy-start | bytes 3145732
  1536.1 4.0 copy-start.2
  1726.6 5.2 copy-start.9
  1731.8 3.9 copy-start.8
  1735.7 161.5 %copy-start.5 = (bf16[256,2048]{1,0:T(8,128)(2,1)S(1)}, bf16[256,2048]{1,0:T(8,128)(2,1)}, u32[]{:S(2)}) copy-start(bf16[256,2048]{1,0:T(8,128)(2,1)} %param.23) | copy-start | bytes 3145732
  1735.7 161.5 %copy-start.13 = (f32[2048]{0:T(1024)S(1)}, f32[2048]{0:T(1024)}, u32[]{:S(2)}) copy-start(f32[2048]{0:T(1024)} %copy-done.12) | copy-start | bytes 24580
  1735.7 161.5 %copy-start.16 = (f32[256]{0:T(256)S(1)}, f32[256]{0:T(256)}, u32[]{:S(2)}) copy-start(f32[256]{0:T(256)} %copy-done.15) | copy-start | bytes 3076
  1739.2 163.1 %copy-start.14 = (f32[2048]{0:T(1024)S(1)}, f32[2048]{0:T(1024)}, u32[]{:S(2)}) copy-start(f32[2048]{0:T(1024)} %get-tuple-element.1394) | copy-start | bytes 24580
  1739.3 203.1 %copy-start.17 = (f32[256]{0:T(256)S(1)}, f32[256]{0:T(256)}, u32[]{:S(2)}) copy-start(f32[256]{0:T(256)} %get-tuple-element.1493) | copy-start | bytes 3076
  1942.3 288.8 %copy-start.1 = (bf16[768,2048]{1,0:T(8,128)(2,1)S(1)}, bf16[768,2048]{1,0:T(8,128)(2,1)}, u32[]{:S(2)}) copy-start(bf16[768,2048]{1,0:T(8,128)(2,1)} %param.33) | copy-start | bytes 9437188
Sparse Core Ops, SparseCore 0:
  11.0 78.5 all-gather.9
  92.5 63.9 all-gather.13
  158.1 80.9 all-gather.7
  241.1 32.3 all-gather.11
  432.5 169.6 reduce-scatter.7
  607.1 80.4 all-gather.15
  689.8 80.5 all-gather.17
  813.7 166.7 reduce-scatter.11
  982.8 87.9 reduce-scatter.9
  1075.6 80.4 all-gather.19
  1470.8 63.3 reduce-scatter.15
  1538.4 188.0 all-reduce.14
  1728.9 168.2 reduce-scatter.13
  1899.9 156.3 reduce-scatter.19
  2062.8 168.3 reduce-scatter.17
where the time goes:
time: 2250 us; the launch traced here: 2240 us
  waiting for transfers between devices  1470 us (65%)
  matrix products  430 us (19%)
  other arithmetic  110 us (5%)
  blocking collectives  91.9 us (4%)
  local copies, waits for them, and re-layouts  82.2 us (4%)
  loops' own time  36 us (2%)
    psum x1, waiting for transfers between devices, on_device(): lax.psum(gate_grad.astype(jnp.bfloat16), 'rows').astype(jnp.float32)  180 us
    reduce_scatter x1, waiting for transfers between devices, on_device(): lax.psum_scatter(qkv_grad_full, ('rows', 'mp'), scatter_dimension=0, tile...  175 us
    reduce_scatter x1, waiting for transfers between devices, on_device(): lax.psum_scatter(attn_partial, 'mp', scatter_dimension=0, tiled=True)  170 us
    reduce_scatter x1, waiting for transfers between devices, on_device(): lax.psum_scatter(input_partial, 'mp', scatter_dimension=0, tiled=True)  158 us
    reduce_scatter x1, waiting for transfers between devices, on_device(): lax.psum_scatter(mid_partial, 'mp', scatter_dimension=0, tiled=True)  156 us
    reduce_scatter x1, waiting for transfers between devices, on_device(): lax.psum_scatter(o_grad_w, ('rows', 'mp'), scatter_dimension=0, tiled=True)  109 us
    reduce_scatter x1, waiting for transfers between devices, on_device(): lax.psum_scatter(ffn_part.astype(jnp.bfloat16), 'mp', scatter_dimension=0...  87.6 us
    all_gather x1, waiting for transfers between devices, on_device(): lax.all_gather(normed_one, 'mp', axis=0, tiled=True)  82.6 us
  transfers between devices with their start and end apart: 15, of which 15 were waited for; matrix products, arithmetic and copies ran while one was open for 6% of the time, Pallas kernels for 0%

commit v1 on v0

--- a/solution.py
+++ b/solution.py
@@ -154,7 +154,12 @@
     seq_scale = weight_seq * sequences_all / (corpora_count * count_seq)
     qkv_full, out_full, gain_one, gain_two = (
         lax.all_gather(qkv_weight, ("rows", "mp"), axis=0, tiled=True),
-        lax.all_gather(out_weight, ("rows", "mp"), axis=0, tiled=True),
+        jnp.concatenate(
+            lax.all_to_all(
+                jnp.stack([out_weight] * lax.axis_size(("rows", "mp"))), ("rows", "mp"), 0, 0
+            ),
+            axis=0,
+        ),
         lax.all_gather(attn_gain, ("rows", "mp"), axis=0, tiled=True),
         lax.all_gather(ffn_gain, ("rows", "mp"), axis=0, tiled=True),
     )

time: 2250 us -> 2270 us (level)
    all_to_all x0 -> x1, waiting for transfers between devices: none -> 135 us  [on_device(): lax.all_to_all(jnp.stack([out_weight] * lax.axis_size(('rows', 'mp'))), (...]
    all_gather x1, waiting for transfers between devices: 82.6 us -> 0.01 us  [on_device(): lax.all_gather(normed_one, 'mp', axis=0, tiled=True)]
    all_gather x1 -> x0, waiting for transfers between devices: 58.8 us -> none  [on_device(): lax.all_gather(out_weight, ('rows', 'mp'), axis=0, tiled=True)]
    all_gather x1, waiting for transfers between devices: 29.9 us -> 58.4 us  [on_device(): lax.all_gather(qkv_weight, ('rows', 'mp'), axis=0, tiled=True)]
  transfers between devices with their start and end apart: 15 -> 15, of which waited for: 15 -> 14; matrix products, arithmetic and copies ran while one was open for 6% -> 6% of each run, Pallas kernels for 0% -> 0%
where the time goes in v1:
time: 2270 us; the launch traced here: 2260 us
  waiting for transfers between devices  1490 us (66%)
  matrix products  429 us (19%)
  other arithmetic  110 us (5%)
  blocking collectives  91.4 us (4%)
  local copies, waits for them, and re-layouts  85.3 us (4%)
  loops' own time  36.2 us (2%)
    psum x1, waiting for transfers between devices, on_device(): lax.psum(gate_grad.astype(jnp.bfloat16), 'rows').astype(jnp.float32)  180 us
    reduce_scatter x1, waiting for transfers between devices, on_device(): lax.psum_scatter(qkv_grad_full, ('rows', 'mp'), scatter_dimension=0, tile...  175 us
    reduce_scatter x1, waiting for transfers between devices, on_device(): lax.psum_scatter(attn_partial, 'mp', scatter_dimension=0, tiled=True)  170 us
    reduce_scatter x1, waiting for transfers between devices, on_device(): lax.psum_scatter(input_partial, 'mp', scatter_dimension=0, tiled=True)  158 us
    reduce_scatter x1, waiting for transfers between devices, on_device(): lax.psum_scatter(mid_partial, 'mp', scatter_dimension=0, tiled=True)  156 us
    all_to_all x1, waiting for transfers between devices, on_device(): lax.all_to_all(jnp.stack([out_weight] * lax.axis_size(('rows', 'mp'))), (...  135 us
    reduce_scatter x1, waiting for transfers between devices, on_device(): lax.psum_scatter(o_grad_w, ('rows', 'mp'), scatter_dimension=0, tiled=True)  109 us
    reduce_scatter x1, waiting for transfers between devices, on_device(): lax.psum_scatter(ffn_part.astype(jnp.bfloat16), 'mp', scatter_dimension=0...  87.5 us
  transfers between devices with their start and end apart: 15, of which 14 were waited for; matrix products, arithmetic and copies ran while one was open for 6% of the time, Pallas kernels for 0%

profile of v1, /device:TPU:0, one launch (start us, length us, event | category | flops | bytes accessed | tf_op | source)
XLA Modules:
  0.0 2263.0 jit_solution(7586262063640482584)
XLA Ops:
  9.9 42.5 %all-reduce.11 = (bf16[2048]{0:T(1024)(128)(2,1)S(1)}, bf16[2048]{0:T(1024)(128)(2,1)S(1)}) all-reduce(bf16[2048]{0:T(1024)(128)(2,1)S(1)} %dynamic-update-slice, bf16[2048]{0:T(1024)(128)(2,1)S(1)} %dynamic-update-slice.1), channel_id=1, replica_groups=mesh['rows'=4,'mp'=8] {'rows','mp'}, use_global_device_ids=true, to_apply=%add.6 | all-reduce | flops 4096 | bytes 16384
  66.1 58.4 %all-gather.9.cloned.1.call-done = bf16[2048,1920]{1,0:T(8,128)(2,1)} async-done(((bf16[64,1920]{1,0:T(8,128)(2,1)}), bf16[2048,1920]{1,0:T(8,128)(2,1)}) %all-gather.9.cloned.1.call-update) | async-done | bytes 7864336 | tf_op jit(solution)/shard_map/all_gather | solution.py:156
  132.6 134.5 %all-to-all-done = bf16[32,40,2048]{2,1,0:T(8,128)(2,1)} async-done(((bf16[32,40,2048]{2,1,0:T(8,128)(2,1)}), bf16[32,40,2048]{2,1,0:T(8,128)(2,1)}, u32[]{:S(2)}, u32[]{:S(2)}) %all-to-all-start) | async-done | bytes 5242912 | tf_op jit(solution)/shard_map/all_to_all | solution.py:158
  267.1 32.0 %all-gather.11.cloned.1.call-done = bf16[2048,640]{1,0:T(8,128)(2,1)} async-done(((bf16[256,640]{1,0:T(8,128)(2,1)}), bf16[2048,640]{1,0:T(8,128)(2,1)}) %all-gather.11.cloned.1.call-update) | async-done | bytes 2621456 | tf_op jit(solution)/shard_map/all_gather | solution.py:175
  299.2 7.9 broadcast.484.clone
  307.0 150.9 %while.42 = (s32[]{:T(128)}, f32[2048,2048]{1,0:T(8,128)}, bf16[10,512,64]{1,2,0:T(8,128)(2,1)}, bf16[10,512,64]{1,2,0:T(8,128)(2,1)}, f32[10,512]{1,0:T(8,128)S...) while((s32[]{:T(128)}, f32[2048,2048]{1,0:T(8,128)}, ...), condition=%wide.region_14.15_spmd, body=%wide.region_1.14_spmd.sunk | while | flops 547767360 | bytes 25982072 | solution.py:207
  340.5 5.5 conditional.17
  356.1 6.2 conditional.17
  401.4 5.5 conditional.17
  416.9 6.2 conditional.17
  458.0 169.8 %reduce-scatter.8.cloned.1.call-done = f32[256,2048]{1,0:T(8,128)} async-done(((f32[2048,2048]{1,0:T(8,128)}), f32[256,2048]{1,0:T(8,128)}) %reduce-scatter.8.cloned.1.call-update) | async-done | bytes 2097168 | tf_op jit(solution)/shard_map/reduce_scatter | solution.py:210
  633.3 9.9 psum.28
  648.8 64.4 %all-gather.13.cloned.1.call-done = bf16[2048,2048]{1,0:T(8,128)(2,1)} async-done(((bf16[256,2048]{1,0:T(8,128)(2,1)}), bf16[2048,2048]{1,0:T(8,128)(2,1)}) %all-gather.13.cloned.1.call-update) | async-done | bytes 8388624 | tf_op jit(solution)/shard_map/all_gather | solution.py:214
  713.2 11.8 fusion.167
  725.0 8.5 fusion.166
  733.5 62.3 %all-gather.15.cloned.1.call-done = bf16[2048,2048]{1,0:T(8,128)(2,1)} async-done(((bf16[256,2048]{1,0:T(8,128)(2,1)}), bf16[2048,2048]{1,0:T(8,128)(2,1)}) %all-gather.15.cloned.1.call-update) | async-done | bytes 8388624 | tf_op jit(solution)/shard_map/all_gather | solution.py:230
  795.8 15.7 multiply_convert_fusion.2
  811.5 13.3 fusion.168
  824.9 13.8 convolution_add_fusion.2
  838.8 10.8 convolution_convert_fusion
  849.7 156.0 %reduce-scatter.12.cloned.1.call-done = f32[256,2048]{1,0:T(8,128)} async-done(((f32[2048,2048]{1,0:T(8,128)}), f32[256,2048]{1,0:T(8,128)}) %reduce-scatter.12.cloned.1.call-update) | async-done | bytes 2097168 | tf_op jit(solution)/shard_map/reduce_scatter | solution.py:246
  1008.4 87.5 %reduce-scatter.10.cloned.1.call-done = bf16[256,2048]{1,0:T(8,128)(2,1)} async-done(((bf16[2048,2048]{1,0:T(8,128)(2,1)}), bf16[256,2048]{1,0:T(8,128)(2,1)}) %reduce-scatter.10.cloned.1.call-update) | async-done | bytes 1048592 | tf_op jit(solution)/shard_map/reduce_scatter | solution.py:219
  1103.0 78.2 %all-gather.17.cloned.1.call-done = bf16[2048,2048]{1,0:T(8,128)(2,1)} async-done(((bf16[256,2048]{1,0:T(8,128)(2,1)}), bf16[2048,2048]{1,0:T(8,128)(2,1)}) %all-gather.17.cloned.1.call-update) | async-done | bytes 8388624 | tf_op jit(solution)/shard_map/all_gather | solution.py:254
  1189.4 5.3 broadcast_in_dim.138
  1194.7 7.9 broadcast.484
  1202.6 293.4 %while.43 = (s32[]{:T(128)}, f32[2048,2048]{1,0:T(8,128)}, f32[2048,640]{0,1:T(8,128)}, f32[2048,1280]{0,1:T(8,128)}, f32[1280,2048]{1,0:T(8,128)}, /*index=5*/s...) while((s32[]{:T(128)}, f32[2048,2048]{1,0:T(8,128)}, ...), condition=%wide.region_32.33_spmd, body=%wide.region_23.32_spmd.sunk | while | flops 1220625536 | bytes 55792484 | solution.py:303
  1208.4 6.6 conditional.18
  1236.0 7.9 conditional.18
  1264.9 9.2 conditional.18
  1295.1 10.5 conditional.18
  1326.6 6.6 conditional.18
  1354.1 7.9 conditional.18
  1383.0 9.2 conditional.18
  1413.2 10.5 conditional.18
  1444.7 6.6 conditional.18
  1472.2 7.9 conditional.18
  1496.1 12.2 convolution_convert_fusion.1
  1508.3 8.5 convolution_convert_fusion.2
  1516.7 8.5 convolution_convert_fusion.3
  1526.6 11.6 copy.61
  1538.2 21.3 reduce-scatter.16.cloned.1.call-done
  1565.5 6.3 pad_maximum_fusion.4
  1571.8 180.3 %all-reduce.15.cloned.1.call-done = (bf16[2048,768]{1,0:T(8,128)(2,1)}, bf16[2048,768]{1,0:T(8,128)(2,1)}, bf16[768,2048]{1,0:T(8,128)(2,1)}) async-done(((bf16[2048,768]{1,0:T(8,128)(2,1)}, bf16[2048,768]{1,0:T(8,128)(2,1)}, bf16[768,2048]{1,0:T(8,128)(2,1)}), (bf16[2048,768]{1,0:T(8,128)(2,1)}, bf16[2048,768]{1,0:T(8,128)(2,1)}, bf16[768,2048]{1,0:T(8,128)(2,1)})) %all-reduce.15.cloned.1.call-update) | async-done | bytes 9437200 | tf_op jit(solution)/shard_map/psum | solution.py:338
  1752.1 5.2 convert_element_type.262
  1764.7 157.8 %reduce-scatter.14.cloned.1.call-done = f32[256,2048]{1,0:T(8,128)} async-done(((f32[2048,2048]{1,0:T(8,128)}), f32[256,2048]{1,0:T(8,128)}) %reduce-scatter.14.cloned.1.call-update) | async-done | bytes 2097168 | tf_op jit(solution)/shard_map/reduce_scatter | solution.py:307
  1927.7 39.0 %all-reduce.10 = (f32[2048]{0:T(1024)S(1)}, f32[2048]{0:T(1024)S(1)}) all-reduce(f32[2048]{0:T(1024)S(1)} %get-tuple-element.1396, f32[2048]{0:T(1024)S(1)} %copy-done.15), channel_id=9, replica_groups=mesh['rows'=4,'mp'=8] {'rows','mp'}, use_global_device_ids=true, to_apply=%region_42.43.clone | all-reduce | flops 4096 | bytes 32768
  1972.5 109.3 %reduce-scatter.20.cloned.1.call-done = f32[40,2048]{1,0:T(8,128)} async-done(((f32[1280,2048]{1,0:T(8,128)}), f32[40,2048]{1,0:T(8,128)}) %reduce-scatter.20.cloned.1.call-update) | async-done | bytes 327696 | tf_op jit(solution)/shard_map/reduce_scatter | solution.py:333
  2081.8 174.5 %reduce-scatter.18.cloned.1.call-done = f32[64,1920]{1,0:T(8,128)} async-done(((f32[2048,1920]{1,0:T(8,128)}), f32[64,1920]{1,0:T(8,128)}) %reduce-scatter.18.cloned.1.call-update) | async-done | bytes 491536 | tf_op jit(solution)/shard_map/reduce_scatter | solution.py:332
  (484 shorter events, 512.8 us)
Async XLA Ops:
  7.2 788.6 %copy-start = (bf16[768,2048]{1,0:T(8,128)(2,1)S(1)}, bf16[768,2048]{1,0:T(8,128)(2,1)}, u32[]{:S(2)}) copy-start(bf16[768,2048]{1,0:T(8,128)(2,1)} %param.33) | copy-start | bytes 9437188
  7.2 50.4 %copy-start.12 = (bf16[40,2048]{1,0:T(8,128)(2,1)S(1)}, bf16[40,2048]{1,0:T(8,128)(2,1)}, u32[]{:S(2)}) copy-start(bf16[40,2048]{1,0:T(8,128)(2,1)} %param.29) | copy-start | bytes 491524
  7.2 117.3 %all-gather.9.cloned.1.call-start = ((), (), s32[]{:S(2)}) async-start(), calls=%async_computation.9 | async-start | bytes 8110080 | tf_op jit(solution)/shard_map/all_gather | solution.py:156
  7.9 259.2 %all-gather.7.cloned.1.call-start = ((), (), s32[]{:S(2)}) async-start(), calls=%async_computation.8 | async-start | bytes 9437184 | tf_op jit(solution)/shard_map/all_gather | solution.py:174
  52.4 2.1 copy-start.13
  54.4 0.5 copy-start.16
  60.6 206.5 %all-to-all-start = ((bf16[32,40,2048]{2,1,0:T(8,128)(2,1)}), bf16[32,40,2048]{2,1,0:T(8,128)(2,1)}, u32[]{:S(2)}, u32[]{:S(2)}) async-start(bf16[32,40,2048]{2,1,0:T(8,128)(2,1)} %stack.2), calls=%async_computation | async-start | bytes 10485760 | tf_op jit(solution)/shard_map/all_to_all | solution.py:158
  65.2 234.0 %all-gather.11.cloned.1.call-start = ((), (), s32[]{:S(2)}) async-start(), calls=%async_computation.10 | async-start | bytes 2949120 | tf_op jit(solution)/shard_map/all_gather | solution.py:175
  132.2 495.6 %reduce-scatter.8.cloned.1.call-start = ((), (), s32[]{:S(2)}) async-start(), calls=%async_computation.11 | async-start | bytes 18874368 | tf_op jit(solution)/shard_map/reduce_scatter | solution.py:210
  458.0 255.2 %all-gather.13.cloned.1.call-start = ((), (), s32[]{:S(2)}) async-start(), calls=%async_computation.12 | async-start | bytes 9437184 | tf_op jit(solution)/shard_map/all_gather | solution.py:214
  630.0 1.3 copy-start.3
  630.0 13.1 copy-start.24
  632.6 163.2 %all-gather.15.cloned.1.call-start = ((), (), s32[]{:S(2)}) async-start(), calls=%async_computation.14 | async-start | bytes 9437184 | tf_op jit(solution)/shard_map/all_gather | solution.py:230
  648.2 357.4 %reduce-scatter.12.cloned.1.call-start = ((), (), s32[]{:S(2)}) async-start(), calls=%async_computation.15 | async-start | bytes 18874368 | tf_op jit(solution)/shard_map/reduce_scatter | solution.py:246
  713.2 11.8 copy-start.19
  713.2 11.8 copy-start.21
  795.8 15.7 copy-start.22
  811.5 13.3 copy-start.25
  811.5 13.3 copy-start.23
  838.7 257.2 %reduce-scatter.10.cloned.1.call-start = ((), (), s32[]{:S(2)}) async-start(), calls=%async_computation.13 | async-start | bytes 9437184 | tf_op jit(solution)/shard_map/reduce_scatter | solution.py:219
  849.6 156.1 %copy-start.4 = (f32[256,2048]{1,0:T(8,128)S(1)}, f32[256,2048]{1,0:T(8,128)}, u32[]{:S(2)}) copy-start(f32[256,2048]{1,0:T(8,128)} %copy-done.3) | copy-start | bytes 6291460
  849.6 246.3 %copy-start.7 = (bf16[256,2048]{1,0:T(8,128)(2,1)S(1)}, bf16[256,2048]{1,0:T(8,128)(2,1)}, u32[]{:S(2)}) copy-start(bf16[256,2048]{1,0:T(8,128)(2,1)} %param.24) | copy-start | bytes 3145732
  849.6 331.6 %all-gather.17.cloned.1.call-start = ((), (), s32[]{:S(2)}) async-start(), calls=%async_computation.16 | async-start | bytes 9437184 | tf_op jit(solution)/shard_map/all_gather | solution.py:254
  1100.6 458.9 %reduce-scatter.16.cloned.1.call-start = ((), (), s32[]{:S(2)}) async-start(), calls=%async_computation.18 | async-start | bytes 5898240 | tf_op jit(solution)/shard_map/reduce_scatter | solution.py:308
  1496.0 12.2 copy-start.26
  1496.0 256.0 %all-reduce.15.cloned.1.call-start = ((), (), s32[]{:S(2)}) async-start(), calls=%async_computation.21 | async-start | bytes 18874368 | tf_op jit(solution)/shard_map/psum | solution.py:338
  1496.1 12.2 copy-start.20
  1508.3 8.5 copy-start.27
  1525.2 397.3 %reduce-scatter.14.cloned.1.call-start = ((), (), s32[]{:S(2)}) async-start(), calls=%async_computation.17 | async-start | bytes 18874368 | tf_op jit(solution)/shard_map/reduce_scatter | solution.py:307
  1525.8 555.9 %reduce-scatter.20.cloned.1.call-start = ((), (), s32[]{:S(2)}) async-start(), calls=%async_computation.20 | async-start | bytes 10813440 | tf_op jit(solution)/shard_map/reduce_scatter | solution.py:333
  1526.6 729.7 %reduce-scatter.18.cloned.1.call-start = ((), (), s32[]{:S(2)}) async-start(), calls=%async_computation.19 | async-start | bytes 16220160 | tf_op jit(solution)/shard_map/reduce_scatter | solution.py:332
  1526.6 34.9 %copy-start.10 = (f32[256,32]{0,1:T(8,128)S(1)}, f32[256,32]{0,1:T(8,128)}, u32[]{:S(2)}) copy-start(f32[256,32]{0,1:T(8,128)} %get-tuple-element.1491) | copy-start | bytes 98308
  1526.6 34.9 %copy-start.11 = (f32[256,32]{0,1:T(8,128)S(1)}, f32[256,32]{0,1:T(8,128)}, u32[]{:S(2)}) copy-start(f32[256,32]{0,1:T(8,128)} %get-tuple-element.1492) | copy-start | bytes 98308
  1526.6 34.9 %copy-start.6 = (bf16[256,2048]{1,0:T(8,128)(2,1)S(1)}, bf16[256,2048]{1,0:T(8,128)(2,1)}, u32[]{:S(2)}) copy-start(bf16[256,2048]{1,0:T(8,128)(2,1)} %fusion.148) | copy-start | bytes 3145732
  1561.5 4.0 copy-start.2
  1752.1 5.2 copy-start.9
  1757.3 3.8 copy-start.8
  1761.1 161.4 %copy-start.5 = (bf16[256,2048]{1,0:T(8,128)(2,1)S(1)}, bf16[256,2048]{1,0:T(8,128)(2,1)}, u32[]{:S(2)}) copy-start(bf16[256,2048]{1,0:T(8,128)(2,1)} %param.23) | copy-start | bytes 3145732
  1761.1 161.4 %copy-start.14 = (f32[2048]{0:T(1024)S(1)}, f32[2048]{0:T(1024)}, u32[]{:S(2)}) copy-start(f32[2048]{0:T(1024)} %copy-done.13) | copy-start | bytes 24580
  1761.2 161.4 %copy-start.17 = (f32[256]{0:T(256)S(1)}, f32[256]{0:T(256)}, u32[]{:S(2)}) copy-start(f32[256]{0:T(256)} %copy-done.16) | copy-start | bytes 3076
  1764.7 162.9 %copy-start.15 = (f32[2048]{0:T(1024)S(1)}, f32[2048]{0:T(1024)}, u32[]{:S(2)}) copy-start(f32[2048]{0:T(1024)} %get-tuple-element.1394) | copy-start | bytes 24580
  1764.7 203.1 %copy-start.18 = (f32[256]{0:T(256)S(1)}, f32[256]{0:T(256)}, u32[]{:S(2)}) copy-start(f32[256]{0:T(256)} %get-tuple-element.1493) | copy-start | bytes 3076
  1967.8 288.5 %copy-start.1 = (bf16[768,2048]{1,0:T(8,128)(2,1)S(1)}, bf16[768,2048]{1,0:T(8,128)(2,1)}, u32[]{:S(2)}) copy-start(bf16[768,2048]{1,0:T(8,128)(2,1)} %param.33) | copy-start | bytes 9437188
Sparse Core Ops, SparseCore 0:
  11.1 113.3 all-gather.8
  126.1 138.7 all-gather.6
  267.1 32.0 all-gather.10
  458.1 169.6 reduce-scatter.7
  632.7 80.4 all-gather.12
  715.2 80.5 all-gather.14
  838.8 166.7 reduce-scatter.11
  1007.9 87.9 reduce-scatter.9
  1100.7 80.4 all-gather.16
  1496.1 63.3 reduce-scatter.15
  1563.9 188.0 all-reduce.14
  1754.3 168.2 reduce-scatter.13
  1925.4 156.2 reduce-scatter.19
  2088.2 168.0 reduce-scatter.17
